TPU v7x, 128 devices: a whole 4x4x4 slice. The times are simulated.
128 devices in a mesh: rows: 8 (over z, core), cols: 16 (over y, x).
Axes of the slice: x: 4, y: 4, z: 4, core: 2. Of those that a mesh axis runs over, the one named last changes fastest.
Arguments:
- model_dir: float32 [131072, 128], P('cols'), may hold values from -6 to 6
- sens_blocks: bfloat16 [8, 6144, 128, 128], P('rows', 'cols'), may hold values from -0.0625 to 0.0625
- blk_row: int32 [8, 6144], P('rows', 'cols'), may hold values from 0 to 31, as said below
- blk_col: int32 [8, 6144], P('rows', 'cols'), may hold values from 0 to 63, as said below
- blk_count: int32 [8, 16], P('rows', 'cols'), may hold values from 48 to 384, as said below
- send_order: int32 [16, 64], P('cols'), may hold values from 0 to 63, each once within a row
- neighbors: int32 [4, 131072], P(None, 'cols'), may hold values from 0 to 131071, as said below
- face_weight: float32 [4, 131072], P(None, 'cols'), may hold values from 0.05 to 0.5
Outputs:
- data_image: float32 [32768, 128], P('rows')
- normal_product: float32 [131072, 128], P('cols')
Inputs may be any that keep to these rules, and one draw needn't show every extreme that they name: Within one device's 384 slots the pairs (blk_row, blk_col) are all different. `blk_col`: paired with blk_row as stated there. The live slots of a device are its first blk_count slots; some device has all 384 live. `send_order`: each row is a permutation. `neighbors`: every neighbour lies within 64 of the cell's own number.
All inputs are finite; a program needn't handle non-finite values.
Results may differ from a plain program's by a relative error of at most 0.0029.
Values may be sent and summed in bfloat16 or wider, within the bound.
A program may use at most 192 MiB of HBM per device.

v0:
```python
import math
import jax
import jax.numpy as jnp
from jax import lax
from jax.sharding import PartitionSpec as P

BLK = 128
RB_DEV = 32
RIM = 64


def padded_2(block, sides, width):
    for axis, dim in sides:
        count = lax.axis_size(axis)
        forward = [(i, i + 1) for i in range(count - 1)]
        backward = [(target, source) for source, target in forward]
        low = lax.ppermute(
            lax.slice_in_dim(block, block.shape[dim] - width, None, axis=dim), axis, forward
        )
        high = lax.ppermute(lax.slice_in_dim(block, 0, width, axis=dim), axis, backward)
        block = jnp.concatenate([low, block, high], axis=dim)
    return block


def haar_matrix(order_n):
    matrix = jnp.ones((1, 1), jnp.float32)
    factor = 1.0 / math.sqrt(2.0)
    while matrix.shape[0] < order_n:
        length = matrix.shape[0]
        upper_half = jnp.kron(matrix, jnp.array([[1.0, 1.0]], jnp.float32))
        lower_half = jnp.kron(
            jnp.eye(length, dtype=jnp.float32), jnp.array([[1.0, -1.0]], jnp.float32)
        )
        matrix = jnp.concatenate([upper_half, lower_half], axis=0) * factor
    return matrix


def one_hot(indices, length, dtype):
    return (indices[:, None] == lax.iota(jnp.int32, length)[None, :]).astype(dtype)


def smoothing(extended, center, neighbors, face_weight, offset):
    cell_count, width = center.shape
    tile_count = cell_count // BLK
    tiles = extended.reshape(tile_count + 1, BLK, width)
    window = jnp.concatenate([tiles[:-1], tiles[1:]], axis=1)
    starts = lax.iota(jnp.int32, tile_count) * BLK
    local_index = (neighbors - offset).reshape(4, tile_count, BLK) - starts[None, :, None]
    span = lax.iota(jnp.int32, 2 * BLK)
    weights = jnp.zeros((tile_count, BLK, 2 * BLK), jnp.float32)
    for face in range(4):
        face_w = face_weight[face].reshape(tile_count, BLK)
        weights = weights + jnp.where(
            local_index[face][:, :, None] == span[None, None, :], face_w[:, :, None], 0.0
        )
    mixed = jnp.einsum("bij,bjn->bin", weights, window, precision=lax.Precision.HIGHEST)
    total_w = jnp.sum(face_weight, axis=0)
    return total_w[:, None] * center - mixed.reshape(cell_count, width)


def synthesize(haar_basis, returned, send_onehot, block_count, cell_count):
    share_cols = returned.shape[-1]
    flat_back = returned.reshape(block_count, BLK * share_cols)
    cell_side = jnp.einsum("jb,jm->bm", send_onehot, flat_back, precision=lax.Precision.HIGHEST)
    cell_side = cell_side.reshape(block_count, BLK, share_cols)
    result = jnp.einsum("ji,bjn->bin", haar_basis, cell_side, precision=lax.Precision.HIGHEST)
    return result.reshape(cell_count, share_cols)


def local(model_dir, sens_blocks, blk_row, blk_col, blk_count, send_order, neighbors, face_weight):
    highest = lax.Precision.HIGHEST
    cell_count, vec_width = model_dir.shape
    block_count = cell_count // BLK
    col_devices = lax.axis_size("cols")
    per_peer = block_count // col_devices
    haar_basis = jnp.asarray(haar_matrix(BLK), jnp.float32)
    cell_blocks = model_dir.reshape(block_count, BLK, vec_width)
    coeffs = jnp.einsum("ij,bjn->bin", haar_basis, cell_blocks, precision=highest).astype(
        jnp.bfloat16
    )
    order_here = send_order[0]
    send_half = one_hot(order_here, block_count, jnp.bfloat16)
    ordered = jnp.dot(
        send_half, coeffs.reshape(block_count, BLK * vec_width), preferred_element_type=jnp.float32
    )
    outgoing = ordered.astype(jnp.bfloat16).reshape(col_devices, per_peer * BLK, vec_width)
    wavelet = lax.all_to_all(outgoing, "cols", split_axis=0, concat_axis=0, tiled=True).reshape(
        block_count, BLK * vec_width
    )
    rows_here = blk_row[0]
    cols_here = blk_col[0]
    sensors = sens_blocks[0]
    slot_count = sensors.shape[0]
    live_slot = lax.iota(jnp.int32, slot_count) < blk_count[0, 0]
    pick_cols = one_hot(cols_here, block_count, jnp.bfloat16)
    picked = jnp.dot(pick_cols, wavelet, preferred_element_type=jnp.float32).astype(jnp.bfloat16)
    picked = picked.reshape(slot_count, BLK, vec_width)
    forward = jnp.einsum("kij,kjn->kin", sensors, picked, preferred_element_type=jnp.float32)
    row_mask = (one_hot(rows_here, RB_DEV, jnp.float32) * live_slot[:, None].astype(jnp.float32)).T
    partial_rows = jnp.dot(
        row_mask, forward.reshape(slot_count, BLK * vec_width), precision=highest
    )
    partial_rows = partial_rows.reshape(RB_DEV, BLK, vec_width)
    predicted = lax.psum(partial_rows, "cols")
    data_image = predicted.reshape(RB_DEV * BLK, vec_width)
    image_half = predicted.astype(jnp.bfloat16).reshape(RB_DEV, BLK * vec_width)
    pick_rows = one_hot(rows_here, RB_DEV, jnp.bfloat16)
    chosen = jnp.dot(pick_rows, image_half, preferred_element_type=jnp.float32).astype(jnp.bfloat16)
    chosen = chosen.reshape(slot_count, BLK, vec_width)
    adjoint = jnp.einsum("kij,kin->kjn", sensors, chosen, preferred_element_type=jnp.float32)
    col_mask = (
        one_hot(cols_here, block_count, jnp.float32) * live_slot[:, None].astype(jnp.float32)
    ).T
    partial_cols = jnp.dot(
        col_mask, adjoint.reshape(slot_count, BLK * vec_width), precision=highest
    )
    partial_cols = partial_cols.reshape(block_count, BLK, vec_width)
    extended = padded_2(model_dir, (("cols", 0),), RIM)
    offset = lax.axis_index("cols") * cell_count - RIM
    send_full = one_hot(order_here, block_count, jnp.float32)
    summed = lax.psum(partial_cols, "rows")
    returned = lax.all_to_all(
        summed.reshape(col_devices, per_peer * BLK, vec_width),
        "cols",
        split_axis=0,
        concat_axis=0,
        tiled=True,
    )
    synthesis = synthesize(haar_basis, returned, send_full, block_count, cell_count)
    normal_product = synthesis + smoothing(extended, model_dir, neighbors, face_weight, offset)
    return (data_image, normal_product)


def solution(mesh):
    placed = (
        P("cols", None),
        P("rows", "cols", None, None),
        P("rows", "cols"),
        P("rows", "cols"),
        P("rows", "cols"),
        P("cols", None),
        P(None, "cols"),
        P(None, "cols"),
    )
    return jax.shard_map(
        local,
        mesh=mesh,
        in_specs=placed,
        out_specs=(P("rows", None), P("cols", None)),
        check_vma=False,
    )
```

profile of v0, /device:TPU:65, one launch (start us, length us, event | category | flops | bytes accessed | tf_op | source)
XLA Modules:
  0.0 500.2 jit_solution(12547211673845322062)
XLA Ops:
  7.3 0.1 copy.30
  7.3 0.7 mul.557
  8.0 0.1 mul.558
  8.2 0.7 mul.541
  8.8 0.1 mul.542
  8.9 0.7 mul.525
  9.6 0.1 mul.526
  9.7 0.7 mul.509
  10.3 0.1 mul.510
  10.4 0.7 mul.493
  11.1 0.1 mul.494
  11.2 0.1 mul.475
  11.2 0.1 mul.476
  11.3 0.7 mul.478
  12.0 0.1 mul.479
  12.1 0.7 mul.468
  12.8 0.1 mul.469
  12.9 0.1 copy.29
  13.0 0.1 broadcast_multiply_fusion.1
  13.1 0.1 broadcast_multiply_fusion.2
  13.2 0.1 broadcast_multiply_fusion.3
  13.3 0.1 broadcast_multiply_fusion.4
  13.3 0.1 maximum_multiply_fusion.4
  13.4 0.1 maximum_multiply_fusion.3
  13.5 0.1 maximum_multiply_fusion.2
  13.6 0.1 maximum_multiply_fusion.1
  13.7 0.1 copy.31
  13.8 6.0 %convolution_convert_fusion.3 = bf16[128,64,128]{2,0,1:T(8,128)(2,1)S(1)} fusion(f32[64,128,128]{2,1,0:T(8,128)} %bitcast.118, f32[64,128]{1,0:T(8,128)S(1)} %broadcast_multiply_fusion, f32[64,128]{1,0:T(8,128)S(1)} %copy.31), kind=kOutput, calls=%fused_computation.50 | convolution fusion | flops 1611694080 | bytes 6356992 | tf_op jit(solution)/shard_map/ij,bjn->bin/dot_general | solution.py:78
  19.9 1.7 convolution_convert_fusion.2
  21.6 2.3 reshape.406
  23.9 6.8 %all-to-all-start = ((bf16[16,512,128]{2,1,0:T(8,128)(2,1)}), bf16[16,512,128]{2,1,0:T(8,128)(2,1)S(1)}, u32[]{:S(2)}, u32[]{:S(2)}) async-start(bf16[16,512,128]{2,1,0:T(8,128)(2,1)} %reshape.406), calls=%async_computation | async-start | bytes 4194304 | tf_op jit(solution)/shard_map/all_to_all | solution.py:87
  30.7 0.5 all-reduce.3.cloned.1.call-start
  31.9 29.3 %all-to-all-done = bf16[16,512,128]{2,1,0:T(8,128)(2,1)S(1)} async-done(((bf16[16,512,128]{2,1,0:T(8,128)(2,1)}), bf16[16,512,128]{2,1,0:T(8,128)(2,1)S(1)}, u32[]{:S(2)}, u32[]{:S(2)}) %all-to-all-start) | async-done | bytes 2097184 | tf_op jit(solution)/shard_map/all_to_all | solution.py:87
  61.2 2.3 reshape.407
  63.4 5.1 %fusion.25 = bf16[48,8,128,128]{3,1,2,0:T(8,128)(2,1)S(1)} fusion(bf16[64,16384]{1,0:T(8,128)(2,1)} %reshape.407, s32[384]{0:T(512)S(1)} %reduce.1), kind=kOutput, calls=%fused_computation.28 | convolution fusion | flops 811622400 | bytes 14681600 | tf_op jit(solution)/shard_map/dot_general | solution.py:96
  68.5 6.5 %copy.49 = bf16[48,8,128,128]{3,2,1,0:T(8,128)(2,1)} copy(bf16[48,8,128,128]{3,1,2,0:T(8,128)(2,1)S(1)} %fusion.25) | data formatting | bytes 25165824
  75.0 22.1 %fusion.8 = f32[384,128,128]{1,2,0:T(8,128)} fusion(bf16[384,128,128]{2,1,0:T(8,128)(2,1)} %bitcast.116, bf16[1,384,128,128]{3,2,1,0:T(8,128)(2,1)} %param.23), kind=kOutput, calls=%fused_computation.11 | convolution fusion | flops 1610612736 | bytes 50331648 | tf_op jit(solution)/shard_map/kij,kjn->kin/dot_general | solution.py:98
  97.1 25.0 %copy.33 = f32[384,128,128]{0,2,1:T(8,128)} copy(f32[384,128,128]{1,2,0:T(8,128)} %fusion.8) | data formatting | bytes 50331648 | tf_op jit(solution)/shard_map/kij,kjn->kin/dot_general | solution.py:98
  122.1 27.2 %fusion.2 = f32[32,128,128]{2,0,1:T(8,128)} fusion(f32[384,128,128]{0,2,1:T(8,128)} %copy.33, f32[384]{0:T(512)S(1)} %fusion.70, s32[384]{0:T(512)S(1)} %reduce), kind=kOutput, calls=%fused_computation.2 | convolution fusion | flops 2415943680 | bytes 27266048 | tf_op jit(solution)/shard_map/dot_general | solution.py:100
  149.3 0.0 all-reduce.5.cloned.1.call-start
  149.4 88.7 %all-reduce.3.cloned.1.call-done = f32[32,128,128]{2,0,1:T(8,128)} async-done(((f32[32,128,128]{2,0,1:T(8,128)}), f32[32,128,128]{2,0,1:T(8,128)}) %all-reduce.3.cloned.1.call-update) | async-done | bytes 2097168 | tf_op jit(solution)/shard_map/psum | solution.py:104
  238.1 9.7 %fusion.26 = bf16[48,8,128,128]{3,1,2,0:T(8,128)(2,1)} fusion(s32[384]{0:T(512)S(1)} %reduce, f32[32,128,128]{2,0,1:T(8,128)} %all-reduce.3.cloned.1.call-done), kind=kOutput, calls=%fused_computation.29 | convolution fusion | flops 409481216 | bytes 14681600 | tf_op jit(solution)/shard_map/dot_general | solution.py:108
  247.8 12.0 %copy.50 = bf16[48,8,128,128]{3,2,1,0:T(8,128)(2,1)} copy(bf16[48,8,128,128]{3,1,2,0:T(8,128)(2,1)} %fusion.26) | data formatting | bytes 25165824
  259.8 13.2 %fusion.11 = f32[384,128,128]{1,2,0:T(8,128)} fusion(bf16[384,128,128]{2,1,0:T(8,128)(2,1)} %bitcast.117, bf16[1,384,128,128]{3,2,1,0:T(8,128)(2,1)S(1)} %bitcast.115), kind=kOutput, calls=%fused_computation.12 | convolution fusion | flops 1610612736 | bytes 50331648 | tf_op jit(solution)/shard_map/kij,kin->kjn/dot_general | solution.py:110
  273.0 25.0 %copy.37 = f32[384,128,128]{0,2,1:T(8,128)} copy(f32[384,128,128]{1,2,0:T(8,128)} %fusion.11) | data formatting | bytes 50331648 | tf_op jit(solution)/shard_map/kij,kin->kjn/dot_general | solution.py:110
  298.0 27.9 %fusion = f32[64,128,128]{2,0,1:T(8,128)S(1)} fusion(f32[384,128,128]{0,2,1:T(8,128)} %copy.37, f32[384]{0:T(512)S(1)} %fusion.70, s32[384]{0:T(512)S(1)} %reduce.1), kind=kOutput, calls=%fused_computation | convolution fusion | flops 4831887360 | bytes 29363200 | tf_op jit(solution)/shard_map/dot_general | solution.py:114
  325.9 4.4 copy.38
  330.3 0.8 fusion.80
  331.1 2.5 collective-permute-start
  333.7 1.3 collective-permute-start.1
  335.0 0.1 bitcast_subtract_fusion.1
  335.1 65.8 %all-reduce.5.cloned.1.call-done = f32[16,512,128]{2,1,0:T(8,128)} async-done(((f32[16,512,128]{2,1,0:T(8,128)}), f32[16,512,128]{2,1,0:T(8,128)}) %all-reduce.5.cloned.1.call-update) | async-done | bytes 4194320 | tf_op jit(solution)/shard_map/psum | solution.py:121
  400.9 6.8 %all-to-all-start.1 = ((f32[16,512,128]{2,1,0:T(8,128)}), f32[16,512,128]{2,1,0:T(8,128)}, u32[]{:S(2)}, u32[]{:S(2)}) async-start(f32[16,512,128]{2,1,0:T(8,128)} %all-reduce.5.cloned.1.call-done), calls=%async_computation.1 | async-start | bytes 8388608 | tf_op jit(solution)/shard_map/all_to_all | solution.py:122
  407.7 0.1 fusion.81
  407.9 0.1 reduce_sum.9
  408.0 4.0 pad_maximum_fusion.1
  412.0 3.8 fusion.93
  415.7 20.2 %fusion.14 = f32[64,128,128]{2,1,0:T(8,128)} fusion(f32[64,128]{1,0:T(8,128)S(1)} %bitcast.134, s32[64,128]{1,0:T(8,128)S(1)} %get-tuple-element.7, f32[64,128]{1,0:T(8,128)S(1)} %bitcast.135, s32[64,128]{1,0:T(8,128)S(1)} %get-tuple-element.8, f32[64,128]{1,0:T(8,128)S(1)} %bitcast.133, s32[64,128]{1,0:T(8,128)S(1)} %get-tuple-element.9, ...), kind=kOutput, calls=%fused_computation.13 | convolution fusion | flops 3244294144 | bytes 12845056 | tf_op jit(solution)/shard_map/bij,bjn->bin/dot_general | solution.py:56
  435.9 2.5 copy.34
  438.4 34.3 %all-to-all-done.1 = f32[16,512,128]{2,1,0:T(8,128)} async-done(((f32[16,512,128]{2,1,0:T(8,128)}), f32[16,512,128]{2,1,0:T(8,128)}, u32[]{:S(2)}, u32[]{:S(2)}) %all-to-all-start.1) | async-done | bytes 4194336 | tf_op jit(solution)/shard_map/all_to_all | solution.py:122
  472.7 4.9 reshape.415
  477.6 4.6 fusion.27
  482.3 6.3 %fusion.30 = f32[64,128,128]{1,2,0:T(8,128)S(1)} fusion(f32[64,128,128]{2,0,1:T(8,128)S(1)} %fusion.27, f32[64,128]{1,0:T(8,128)S(1)} %broadcast_multiply_fusion, f32[64,128]{1,0:T(8,128)S(1)} %copy.31), kind=kOutput, calls=%fused_computation.37 | convolution fusion | flops 1610645504 | bytes 8454144 | tf_op jit(solution)/shard_map/ji,bjn->bin/dot_general | solution.py:66
  488.6 4.6 bitcast_add_fusion
  (52 shorter events, 0.3 us)
Async XLA Ops:
  7.2 12.7 %copy-start.5 = (s32[1,64]{1,0:T(1,128)S(1)}, s32[1,64]{1,0:T(1,128)}, u32[]{:S(2)}) copy-start(s32[1,64]{1,0:T(1,128)} %param.27) | copy-start | bytes 772
  21.6 10.3 %copy-start.6 = (s32[1,384]{1,0:T(1,128)S(1)}, s32[1,384]{1,0:T(1,128)}, u32[]{:S(2)}) copy-start(s32[1,384]{1,0:T(1,128)} %param.25) | copy-start | bytes 4612
  21.6 10.3 %copy-start.7 = (s32[1,384]{1,0:T(1,128)S(1)}, s32[1,384]{1,0:T(1,128)}, u32[]{:S(2)}) copy-start(s32[1,384]{1,0:T(1,128)} %param.24) | copy-start | bytes 4612
  23.9 37.3 %all-to-all-start = ((bf16[16,512,128]{2,1,0:T(8,128)(2,1)}), bf16[16,512,128]{2,1,0:T(8,128)(2,1)S(1)}, u32[]{:S(2)}, u32[]{:S(2)}) async-start(bf16[16,512,128]{2,1,0:T(8,128)(2,1)} %reshape.406), calls=%async_computation | async-start | bytes 4194304 | tf_op jit(solution)/shard_map/all_to_all | solution.py:87
  30.7 207.4 %all-reduce.3.cloned.1.call-start = ((), (), s32[]{:S(2)}) async-start(), calls=%async_computation.2 | async-start | bytes 4194304 | tf_op jit(solution)/shard_map/psum | solution.py:104
  149.3 251.6 %all-reduce.5.cloned.1.call-start = ((), (), s32[]{:S(2)}) async-start(), calls=%async_computation.3 | async-start | bytes 8388608 | tf_op jit(solution)/shard_map/psum | solution.py:121
  238.1 21.7 %slice-start = ((s8[12582912]{0:T(1024)(128)(4,1)}), s8[4194304]{0:T(1024)(128)(4,1)S(1)}, s32[]{:S(2)}) async-start(s8[12582912]{0:T(1024)(128)(4,1)} %bitcast.114), calls=%async_computation.4 | async-start | bytes 8388608
  238.1 21.7 %slice-start.1 = ((s8[12582912]{0:T(1024)(128)(4,1)}), s8[4194304]{0:T(1024)(128)(4,1)S(1)}, s32[]{:S(2)}) async-start(s8[12582912]{0:T(1024)(128)(4,1)} %bitcast.114), calls=%async_computation.5 | async-start | bytes 8388608
  247.8 12.0 %slice-start.2 = ((s8[12582912]{0:T(1024)(128)(4,1)}), s8[4194304]{0:T(1024)(128)(4,1)S(1)}, s32[]{:S(2)}) async-start(s8[12582912]{0:T(1024)(128)(4,1)} %bitcast.114), calls=%async_computation.6 | async-start | bytes 8388608
  330.3 4.7 copy-start.4
  331.1 76.8 %collective-permute-start = (f32[64,128]{1,0:T(8,128)S(1)}, f32[64,128]{1,0:T(8,128)S(1)}, u32[]{:S(2)}, u32[]{:S(2)}) collective-permute-start(f32[64,128]{1,0:T(8,128)S(1)} %get-tuple-element.4), channel_id=1, source_target_pairs={{0,1},{1,2},{2,3},{3,4},{4,5},{5,6},{6,7},{7,8},{8,9},{9,10},{10,1... | collective-permute-start | bytes 98312 | tf_op jit(solution)/shard_map/ppermute | solution.py:17
  333.7 74.3 %collective-permute-start.1 = (f32[64,128]{1,0:T(8,128)S(1)}, f32[64,128]{1,0:T(8,128)S(1)}, u32[]{:S(2)}, u32[]{:S(2)}) collective-permute-start(f32[64,128]{1,0:T(8,128)S(1)} %get-tuple-element.5), channel_id=1, source_target_pairs={{1,0},{2,1},{3,2},{4,3},{5,4},{6,5},{7,6},{8,7},{9,8},{10,9},{11,1... | collective-permute-start | bytes 98312 | tf_op jit(solution)/shard_map/ppermute | solution.py:20
  335.1 72.6 %copy-start.3 = (f32[4,8192]{1,0:T(4,128)S(1)}, f32[4,8192]{1,0:T(4,128)}, u32[]{:S(2)}) copy-start(f32[4,8192]{1,0:T(4,128)} %param.29) | copy-start | bytes 393220
  400.9 71.8 %all-to-all-start.1 = ((f32[16,512,128]{2,1,0:T(8,128)}), f32[16,512,128]{2,1,0:T(8,128)}, u32[]{:S(2)}, u32[]{:S(2)}) async-start(f32[16,512,128]{2,1,0:T(8,128)} %all-reduce.5.cloned.1.call-done), calls=%async_computation.1 | async-start | bytes 8388608 | tf_op jit(solution)/shard_map/all_to_all | solution.py:122
  415.7 20.2 %copy-start.1 = (f32[32,128,128]{2,0,1:T(8,128)S(1)}, f32[32,128,128]{2,0,1:T(8,128)}, u32[]{:S(2)}) copy-start(f32[32,128,128]{2,0,1:T(8,128)} %all-reduce.3.cloned.1.call-done) | copy-start | bytes 6291460
  482.3 6.3 %copy-start = (f32[8192,128]{1,0:T(8,128)S(1)}, f32[8192,128]{1,0:T(8,128)}, u32[]{:S(2)}) copy-start(f32[8192,128]{1,0:T(8,128)} %param.22) | copy-start | bytes 12582916
  482.3 6.3 %copy-start.2 = (f32[64,128,128]{2,1,0:T(8,128)S(1)}, f32[64,128,128]{2,1,0:T(8,128)}, u32[]{:S(2)}) copy-start(f32[64,128,128]{2,1,0:T(8,128)} %fusion.14) | copy-start | bytes 12582916
Sparse Core Ops, SparseCore 0:
  149.4 88.5 all-reduce.2
  330.4 70.4 all-reduce.4
where the time goes:
time: 507 us; the launch traced here: 500 us
  waiting for transfers between devices  218 us (43%)
  matrix products  144 us (28%)
  local copies, waits for them, and re-layouts  91.8 us (18%)
  starting transfers between devices  17.9 us (4%)
  between operations  15.3 us (3%)
  other arithmetic  13.2 us (3%)
    psum x1, waiting for transfers between devices, local(): predicted = lax.psum(partial_rows, 'cols')  88.7 us
    psum x1, waiting for transfers between devices, local(): summed = lax.psum(partial_cols, 'rows')  65.8 us
    all_to_all x1, waiting for transfers between devices, local(): lax.all_to_all(summed.reshape(col_devices, per_peer * BLK, vec_width), 'c...  34.3 us
    all_to_all x1, waiting for transfers between devices, local(): lax.all_to_all(outgoing, 'cols', split_axis=0, concat_axis=0, tiled=True)  29.3 us
    dot_general x1, matrix products, local(): jnp.dot(col_mask, adjoint.reshape(slot_count, BLK * vec_width), precision...  27.9 us
    dot_general x1, matrix products, local(): jnp.dot(row_mask, forward.reshape(slot_count, BLK * vec_width), precision...  27.2 us
    dot_general x1, local copies, waits for them, and re-layouts, local(): jnp.einsum('kij,kin->kjn', sensors, chosen, preferred_element_type=jnp.fl...  25 us
    dot_general x1, local copies, waits for them, and re-layouts, local(): jnp.einsum('kij,kjn->kin', sensors, picked, preferred_element_type=jnp.fl...  25 us
  transfers between devices with their start and end apart: 6, of which 4 were waited for; matrix products, arithmetic and copies ran while one was open for 6% of the time, Pallas kernels for 0%

commit v1 on v0

--- a/solution.py
+++ b/solution.py
@@ -101,7 +101,7 @@
         row_mask, forward.reshape(slot_count, BLK * vec_width), precision=highest
     )
     partial_rows = partial_rows.reshape(RB_DEV, BLK, vec_width)
-    predicted = lax.psum(partial_rows, "cols")
+    predicted = jnp.sum(lax.all_gather(partial_rows, "cols"), axis=0)
     data_image = predicted.reshape(RB_DEV * BLK, vec_width)
     image_half = predicted.astype(jnp.bfloat16).reshape(RB_DEV, BLK * vec_width)
     pick_rows = one_hot(rows_here, RB_DEV, jnp.bfloat16)

time: 507 us -> 626 us (1.23)
  waiting for transfers between devices: 218 us -> 325 us
  other arithmetic: 13.2 us -> 26.3 us
    all_gather x0 -> x1, waiting for transfers between devices: none -> 196 us  [local(): predicted = jnp.sum(lax.all_gather(partial_rows, 'cols'), axis=0)]
    psum x1 -> x0, waiting for transfers between devices: 88.7 us -> none  [local(): predicted = lax.psum(partial_rows, 'cols')]
    reduce_sum x0 -> x1, other arithmetic: none -> 13 us  [local(): predicted = jnp.sum(lax.all_gather(partial_rows, 'cols'), axis=0)]
    unnamed x24 -> x26, local copies, waits for them, and re-layouts: 18.5 us -> 19.9 us
  transfers between devices with their start and end apart: 6 -> 6, of which waited for: 4 -> 4; matrix products, arithmetic and copies ran while one was open for 6% -> 5% of each run, Pallas kernels for 0% -> 0%
where the time goes in v1:
time: 626 us; the launch traced here: 619 us
  waiting for transfers between devices  325 us (52%)
  matrix products  141 us (23%)
  local copies, waits for them, and re-layouts  93.3 us (15%)
  other arithmetic  26.3 us (4%)
  starting transfers between devices  18.4 us (3%)
  between operations  15.4 us (2%)
    all_gather x1, waiting for transfers between devices, local(): predicted = jnp.sum(lax.all_gather(partial_rows, 'cols'), axis=0)  196 us
    psum x1, waiting for transfers between devices, local(): summed = lax.psum(partial_cols, 'rows')  64.7 us
    all_to_all x1, waiting for transfers between devices, local(): lax.all_to_all(summed.reshape(col_devices, per_peer * BLK, vec_width), 'c...  34.5 us
    all_to_all x1, waiting for transfers between devices, local(): lax.all_to_all(outgoing, 'cols', split_axis=0, concat_axis=0, tiled=True)  29.3 us
    dot_general x1, matrix products, local(): jnp.dot(col_mask, adjoint.reshape(slot_count, BLK * vec_width), precision...  28.1 us
    dot_general x1, matrix products, local(): jnp.dot(row_mask, forward.reshape(slot_count, BLK * vec_width), precision...  27.2 us
    dot_general x1, local copies, waits for them, and re-layouts, local(): jnp.einsum('kij,kjn->kin', sensors, picked, preferred_element_type=jnp.fl...  24.9 us
    dot_general x1, local copies, waits for them, and re-layouts, local(): jnp.einsum('kij,kin->kjn', sensors, chosen, preferred_element_type=jnp.fl...  24.9 us
  transfers between devices with their start and end apart: 6, of which 4 were waited for; matrix products, arithmetic and copies ran while one was open for 5% of the time, Pallas kernels for 0%

profile of v1, /device:TPU:65, one launch (start us, length us, event | category | flops | bytes accessed | tf_op | source)
XLA Modules:
  0.0 619.4 jit_solution(9758981362337699916)
XLA Ops:
  7.3 0.7 mul.557
  8.0 0.1 mul.558
  8.2 0.7 mul.541
  8.8 0.1 mul.542
  8.9 0.7 mul.525
  9.6 0.1 mul.526
  9.7 0.7 mul.509
  10.3 0.1 mul.510
  10.4 0.7 mul.493
  11.1 0.1 mul.494
  11.2 0.1 mul.475
  11.2 0.1 mul.476
  11.3 0.7 mul.478
  12.0 0.1 mul.479
  12.1 0.7 mul.468
  12.8 0.1 mul.469
  12.9 0.1 copy.48
  13.0 0.1 broadcast_multiply_fusion.1
  13.1 0.1 broadcast_multiply_fusion.2
  13.2 0.1 broadcast_multiply_fusion.3
  13.3 0.1 broadcast_multiply_fusion.4
  13.3 0.1 maximum_multiply_fusion.4
  13.4 0.1 maximum_multiply_fusion.3
  13.5 0.1 maximum_multiply_fusion.2
  13.6 0.1 maximum_multiply_fusion.1
  13.8 6.0 convolution_convert_fusion.3
  19.9 1.7 convolution_convert_fusion.2
  21.6 2.3 reshape.409
  23.9 6.8 %all-to-all-start = ((bf16[16,512,128]{2,1,0:T(8,128)(2,1)}), bf16[16,512,128]{2,1,0:T(8,128)(2,1)S(1)}, u32[]{:S(2)}, u32[]{:S(2)}) async-start(bf16[16,512,128]{2,1,0:T(8,128)(2,1)} %reshape.409), calls=%async_computation | async-start | bytes 4194304 | tf_op jit(solution)/shard_map/all_to_all | solution.py:87
  30.7 0.5 all-gather.3.cloned.1.call-start
  31.9 29.3 %all-to-all-done = bf16[16,512,128]{2,1,0:T(8,128)(2,1)S(1)} async-done(((bf16[16,512,128]{2,1,0:T(8,128)(2,1)}), bf16[16,512,128]{2,1,0:T(8,128)(2,1)S(1)}, u32[]{:S(2)}, u32[]{:S(2)}) %all-to-all-start) | async-done | bytes 2097184 | tf_op jit(solution)/shard_map/all_to_all | solution.py:87
  61.2 2.3 reshape.410
  63.5 5.1 fusion.25
  68.5 6.5 %copy.68 = bf16[48,8,128,128]{3,2,1,0:T(8,128)(2,1)} copy(bf16[48,8,128,128]{3,1,2,0:T(8,128)(2,1)S(1)} %fusion.25) | data formatting | bytes 25165824
  75.1 22.1 %fusion.8 = f32[384,128,128]{1,2,0:T(8,128)} fusion(bf16[384,128,128]{2,1,0:T(8,128)(2,1)} %bitcast.117, bf16[1,384,128,128]{3,2,1,0:T(8,128)(2,1)} %param.23), kind=kOutput, calls=%fused_computation.11 | convolution fusion | flops 1610612736 | bytes 50331648 | tf_op jit(solution)/shard_map/kij,kjn->kin/dot_general | solution.py:98
  97.2 24.9 %copy.52 = f32[384,128,128]{0,2,1:T(8,128)} copy(f32[384,128,128]{1,2,0:T(8,128)} %fusion.8) | data formatting | bytes 50331648 | tf_op jit(solution)/shard_map/kij,kjn->kin/dot_general | solution.py:98
  122.1 27.2 %fusion.2 = f32[32,128,128]{2,0,1:T(8,128)} fusion(f32[384,128,128]{0,2,1:T(8,128)} %copy.52, f32[384]{0:T(512)S(1)} %fusion.70, s32[384]{0:T(512)S(1)} %reduce), kind=kOutput, calls=%fused_computation.2 | convolution fusion | flops 2415943680 | bytes 27266048 | tf_op jit(solution)/shard_map/dot_general | solution.py:100
  149.3 0.2 all-reduce.2.cloned.1.call-start
  149.5 196.5 %all-gather.3.cloned.1.call-done = f32[512,128,128]{2,0,1:T(8,128)} async-done(((f32[32,128,128]{2,0,1:T(8,128)}), f32[512,128,128]{2,0,1:T(8,128)}) %all-gather.3.cloned.1.call-update) | async-done | bytes 33554448 | tf_op jit(solution)/shard_map/all_gather | solution.py:104
  346.0 13.0 %reduce_sum.18 = f32[32,128,128]{2,0,1:T(8,128)S(1)} reduce(f32[16,32,128,128]{3,1,0,2:T(8,128)} %bitcast.120, f32[]{:T(128)} %constant.8.clone.1), dimensions={0}, to_apply=%region_0.1 | reduce | flops 7864320 | bytes 35651588 | tf_op jit(solution)/shard_map/reduce_sum | solution.py:104
  359.1 1.3 copy-done.1
  360.4 6.5 %fusion.26 = bf16[48,8,128,128]{3,1,2,0:T(8,128)(2,1)} fusion(s32[384]{0:T(512)S(1)} %reduce, f32[32,128,128]{2,0,1:T(8,128)S(1)} %reduce_sum.18), kind=kOutput, calls=%fused_computation.29 | convolution fusion | flops 409481216 | bytes 14681600 | tf_op jit(solution)/shard_map/dot_general | solution.py:108
  366.9 12.0 %copy.69 = bf16[48,8,128,128]{3,2,1,0:T(8,128)(2,1)} copy(bf16[48,8,128,128]{3,1,2,0:T(8,128)(2,1)} %fusion.26) | data formatting | bytes 25165824
  378.9 13.2 %fusion.11 = f32[384,128,128]{1,2,0:T(8,128)} fusion(bf16[384,128,128]{2,1,0:T(8,128)(2,1)} %bitcast.118, bf16[1,384,128,128]{3,2,1,0:T(8,128)(2,1)S(1)} %bitcast.116), kind=kOutput, calls=%fused_computation.12 | convolution fusion | flops 1610612736 | bytes 50331648 | tf_op jit(solution)/shard_map/kij,kin->kjn/dot_general | solution.py:110
  392.1 24.9 %copy.56 = f32[384,128,128]{0,2,1:T(8,128)} copy(f32[384,128,128]{1,2,0:T(8,128)} %fusion.11) | data formatting | bytes 50331648 | tf_op jit(solution)/shard_map/kij,kin->kjn/dot_general | solution.py:110
  417.1 28.1 %fusion = f32[64,128,128]{2,0,1:T(8,128)S(1)} fusion(f32[384,128,128]{0,2,1:T(8,128)} %copy.56, f32[384]{0:T(512)S(1)} %fusion.70, s32[384]{0:T(512)S(1)} %reduce.1), kind=kOutput, calls=%fused_computation | convolution fusion | flops 4831887360 | bytes 29363200 | tf_op jit(solution)/shard_map/dot_general | solution.py:114
  445.2 4.4 copy.57
  449.6 0.8 fusion.80
  450.5 3.1 collective-permute-start
  453.5 1.3 collective-permute-start.1
  454.9 0.1 bitcast_subtract_fusion.1
  455.0 64.7 %all-reduce.2.cloned.1.call-done = f32[16,512,128]{2,1,0:T(8,128)} async-done(((f32[16,512,128]{2,1,0:T(8,128)}), f32[16,512,128]{2,1,0:T(8,128)}) %all-reduce.2.cloned.1.call-update) | async-done | bytes 4194320 | tf_op jit(solution)/shard_map/psum | solution.py:121
  519.7 6.6 %all-to-all-start.1 = ((f32[16,512,128]{2,1,0:T(8,128)}), f32[16,512,128]{2,1,0:T(8,128)}, u32[]{:S(2)}, u32[]{:S(2)}) async-start(f32[16,512,128]{2,1,0:T(8,128)} %all-reduce.2.cloned.1.call-done), calls=%async_computation.1 | async-start | bytes 8388608 | tf_op jit(solution)/shard_map/all_to_all | solution.py:122
  526.3 0.1 fusion.81
  526.4 0.1 reduce_sum.19
  526.5 4.0 pad_maximum_fusion.1
  530.5 3.8 fusion.93
  534.3 20.2 %fusion.14 = f32[64,128,128]{2,1,0:T(8,128)} fusion(f32[64,128]{1,0:T(8,128)S(1)} %bitcast.136, s32[64,128]{1,0:T(8,128)S(1)} %get-tuple-element.7, f32[64,128]{1,0:T(8,128)S(1)} %bitcast.137, s32[64,128]{1,0:T(8,128)S(1)} %get-tuple-element.8, f32[64,128]{1,0:T(8,128)S(1)} %bitcast.135, s32[64,128]{1,0:T(8,128)S(1)} %get-tuple-element.9, ...), kind=kOutput, calls=%fused_computation.13 | convolution fusion | flops 3244294144 | bytes 12845056 | tf_op jit(solution)/shard_map/bij,bjn->bin/dot_general | solution.py:56
  554.4 2.5 copy.53
  557.0 34.5 %all-to-all-done.1 = f32[16,512,128]{2,1,0:T(8,128)} async-done(((f32[16,512,128]{2,1,0:T(8,128)}), f32[16,512,128]{2,1,0:T(8,128)}, u32[]{:S(2)}, u32[]{:S(2)}) %all-to-all-start.1) | async-done | bytes 4194336 | tf_op jit(solution)/shard_map/all_to_all | solution.py:122
  591.5 5.2 reshape.417
  596.6 4.7 fusion.27
  601.4 6.3 %fusion.30 = f32[64,128,128]{1,2,0:T(8,128)S(1)} fusion(f32[64,128,128]{2,0,1:T(8,128)S(1)} %fusion.27, f32[64,128]{1,0:T(8,128)S(1)} %broadcast_multiply_fusion, f32[64,128]{1,0:T(8,128)S(1)} %copy.50), kind=kOutput, calls=%fused_computation.37 | convolution fusion | flops 1610645504 | bytes 8454144 | tf_op jit(solution)/shard_map/ji,bjn->bin/dot_general | solution.py:66
  607.7 4.6 bitcast_add_fusion
  (55 shorter events, 0.5 us)
Async XLA Ops:
  7.2 12.7 %copy-start.6 = (s32[1,64]{1,0:T(1,128)S(1)}, s32[1,64]{1,0:T(1,128)}, u32[]{:S(2)}) copy-start(s32[1,64]{1,0:T(1,128)} %param.27) | copy-start | bytes 772
  21.6 10.3 %copy-start.7 = (s32[1,384]{1,0:T(1,128)S(1)}, s32[1,384]{1,0:T(1,128)}, u32[]{:S(2)}) copy-start(s32[1,384]{1,0:T(1,128)} %param.25) | copy-start | bytes 4612
  21.6 10.3 %copy-start.8 = (s32[1,384]{1,0:T(1,128)S(1)}, s32[1,384]{1,0:T(1,128)}, u32[]{:S(2)}) copy-start(s32[1,384]{1,0:T(1,128)} %param.24) | copy-start | bytes 4612
  23.9 37.3 %all-to-all-start = ((bf16[16,512,128]{2,1,0:T(8,128)(2,1)}), bf16[16,512,128]{2,1,0:T(8,128)(2,1)S(1)}, u32[]{:S(2)}, u32[]{:S(2)}) async-start(bf16[16,512,128]{2,1,0:T(8,128)(2,1)} %reshape.409), calls=%async_computation | async-start | bytes 4194304 | tf_op jit(solution)/shard_map/all_to_all | solution.py:87
  30.7 315.3 %all-gather.3.cloned.1.call-start = ((), (), s32[]{:S(2)}) async-start(), calls=%async_computation.3 | async-start | bytes 35651584 | tf_op jit(solution)/shard_map/all_gather | solution.py:104
  149.3 370.4 %all-reduce.2.cloned.1.call-start = ((), (), s32[]{:S(2)}) async-start(), calls=%async_computation.2 | async-start | bytes 8388608 | tf_op jit(solution)/shard_map/psum | solution.py:121
  359.0 1.3 copy-start.1
  360.4 18.5 %slice-start = ((s8[12582912]{0:T(1024)(128)(4,1)}), s8[4194304]{0:T(1024)(128)(4,1)S(1)}, s32[]{:S(2)}) async-start(s8[12582912]{0:T(1024)(128)(4,1)} %bitcast.115), calls=%async_computation.4 | async-start | bytes 8388608
  360.4 18.5 %slice-start.1 = ((s8[12582912]{0:T(1024)(128)(4,1)}), s8[4194304]{0:T(1024)(128)(4,1)S(1)}, s32[]{:S(2)}) async-start(s8[12582912]{0:T(1024)(128)(4,1)} %bitcast.115), calls=%async_computation.5 | async-start | bytes 8388608
  366.9 12.0 %slice-start.2 = ((s8[12582912]{0:T(1024)(128)(4,1)}), s8[4194304]{0:T(1024)(128)(4,1)S(1)}, s32[]{:S(2)}) async-start(s8[12582912]{0:T(1024)(128)(4,1)} %bitcast.115), calls=%async_computation.6 | async-start | bytes 8388608
  449.6 5.3 copy-start.5
  450.5 76.0 %collective-permute-start = (f32[64,128]{1,0:T(8,128)S(1)}, f32[64,128]{1,0:T(8,128)S(1)}, u32[]{:S(2)}, u32[]{:S(2)}) collective-permute-start(f32[64,128]{1,0:T(8,128)S(1)} %get-tuple-element.4), channel_id=1, source_target_pairs={{0,1},{1,2},{2,3},{3,4},{4,5},{5,6},{6,7},{7,8},{8,9},{9,10},{10,1... | collective-permute-start | bytes 98312 | tf_op jit(solution)/shard_map/ppermute | solution.py:17
  453.5 72.9 %collective-permute-start.1 = (f32[64,128]{1,0:T(8,128)S(1)}, f32[64,128]{1,0:T(8,128)S(1)}, u32[]{:S(2)}, u32[]{:S(2)}) collective-permute-start(f32[64,128]{1,0:T(8,128)S(1)} %get-tuple-element.5), channel_id=1, source_target_pairs={{1,0},{2,1},{3,2},{4,3},{5,4},{6,5},{7,6},{8,7},{9,8},{10,9},{11,1... | collective-permute-start | bytes 98312 | tf_op jit(solution)/shard_map/ppermute | solution.py:20
  455.0 71.3 %copy-start.4 = (f32[4,8192]{1,0:T(4,128)S(1)}, f32[4,8192]{1,0:T(4,128)}, u32[]{:S(2)}) copy-start(f32[4,8192]{1,0:T(4,128)} %param.29) | copy-start | bytes 393220
  519.7 71.8 %all-to-all-start.1 = ((f32[16,512,128]{2,1,0:T(8,128)}), f32[16,512,128]{2,1,0:T(8,128)}, u32[]{:S(2)}, u32[]{:S(2)}) async-start(f32[16,512,128]{2,1,0:T(8,128)} %all-reduce.2.cloned.1.call-done), calls=%async_computation.1 | async-start | bytes 8388608 | tf_op jit(solution)/shard_map/all_to_all | solution.py:122
  534.3 20.2 %copy-start.2 = (f32[32,128,128]{2,0,1:T(8,128)S(1)}, f32[32,128,128]{2,0,1:T(8,128)}, u32[]{:S(2)}) copy-start(f32[32,128,128]{2,0,1:T(8,128)} %copy-done.1) | copy-start | bytes 6291460
  601.4 6.3 %copy-start = (f32[8192,128]{1,0:T(8,128)S(1)}, f32[8192,128]{1,0:T(8,128)}, u32[]{:S(2)}) copy-start(f32[8192,128]{1,0:T(8,128)} %param.22) | copy-start | bytes 12582916
  601.4 6.3 %copy-start.3 = (f32[64,128,128]{2,1,0:T(8,128)S(1)}, f32[64,128,128]{2,1,0:T(8,128)}, u32[]{:S(2)}) copy-start(f32[64,128,128]{2,1,0:T(8,128)} %fusion.14) | copy-start | bytes 12582916
Sparse Core Ops, SparseCore 0:
  149.4 196.5 all-gather.2
  449.8 69.8 all-reduce.1
